TPU v7x, 32 devices: a whole 2x2x4 slice. The times are simulated.
32 devices in a mesh: section: 2 (over x), mirror: 2 (over y), dp: 8 (over z, core).
Axes of the slice: x: 2, y: 2, z: 4, core: 2. Of those that a mesh axis runs over, the one named last changes fastest.
Arguments:
- sent_fwd: bfloat16 [2, 2, 8, 4096], P('section', 'mirror', 'dp'), may hold values from -36 to 36
- sent_bwd: bfloat16 [2, 2, 8, 4096], P('section', 'mirror', 'dp'), may hold values from -6 to 6
- stash: bfloat16 [2, 2, 8, 4096], P('section', 'mirror', 'dp'), may hold values from -36 to 36
- gain: float32 [2, 4096], P('section'), may hold values from 0.5 to 1.5
- w_in: bfloat16 [2, 4096, 1024], P('section', None, 'dp'), may hold values from -0.09375 to 0.09375
- w_out: bfloat16 [2, 1024, 4096], P('section', 'dp'), may hold values from -0.375 to 0.375
Outputs:
- fwd_out: bfloat16 [2, 2, 8, 4096], P('section', 'mirror', 'dp')
- bwd_out: bfloat16 [2, 2, 8, 4096], P('section', 'mirror', 'dp')
- w_in_grad: bfloat16 [2, 4096, 1024], P('section', 'mirror', 'dp')
- w_out_grad: bfloat16 [2, 1024, 4096], P('section', 'dp', 'mirror')
All inputs are finite; a program needn't handle non-finite values.
Results may differ from a plain program's by a relative error of at most 0.0068.
Values may be sent and summed in bfloat16 or wider, within the bound.
No kernel may reach another device: no remote copies, remote signals or barrier semaphores. Data moves between devices by JAX's collectives and lax.ppermute only.
A program may use at most 64 MiB of HBM per device.

v0:
```python
import jax
import jax.numpy as jnp
from jax import lax
from jax.sharding import PartitionSpec as P


def extended_2(block, sides, width):
    for axis, dim in sides:
        count = lax.axis_size(axis)
        forward = [(i, i + 1) for i in range(count - 1)]
        forward.append((count - 1, 0))
        backward = [(target, source) for source, target in forward]
        low = lax.ppermute(
            lax.slice_in_dim(block, block.shape[dim] - width, None, axis=dim), axis, forward
        )
        high = lax.ppermute(lax.slice_in_dim(block, 0, width, axis=dim), axis, backward)
        block = jnp.concatenate([low, block, high], axis=dim)
    return block


def swapped(value, axis, apart):
    mask = 2**apart
    pairs = [(source, source ^ mask) for source in range(lax.axis_size(axis))]
    return lax.ppermute(value, axis, pairs)


def norm_rows(x):
    centre = x - jnp.mean(x, axis=-1, keepdims=True)
    rstd = lax.rsqrt(jnp.mean(centre * centre, axis=-1, keepdims=True) + 1e-05)
    return (centre * rstd, rstd)


def gelu_pair(h):
    coeff = 0.7978845608028654
    inner = coeff * (h + 0.044715 * h * h * h)
    tanh_val = jnp.tanh(inner)
    value = 0.5 * h * (1.0 + tanh_val)
    slope = 0.5 * (1.0 + tanh_val) + 0.5 * h * (1.0 - tanh_val * tanh_val) * coeff * (
        1.0 + 3.0 * 0.044715 * h * h
    )
    return (value, slope)


def rounded(values):
    return lax.optimization_barrier(values.astype(jnp.bfloat16)).astype(jnp.float32)


def on_device(sent_fwd, sent_bwd, stash, gain, w_in, w_out):
    mirror_pos = lax.axis_index("mirror")
    downward = mirror_pos == 0
    fwd_local = sent_fwd[0, 0]
    bwd_local = sent_bwd[0, 0]
    upward_load = jnp.where(downward, fwd_local, bwd_local)
    lower_load = jnp.where(downward, bwd_local, fwd_local)
    block = jnp.stack([lower_load, upward_load])
    extended = extended_2(block, (("section", 0),), 1)
    from_lower = extended[0]
    from_upper = extended[3]
    fwd_in = jnp.where(downward, from_lower, from_upper)
    bwd_in = jnp.where(downward, from_upper, from_lower)
    gain_row = gain[0]
    w_first = w_in[0]
    w_second = w_out[0]
    x_fwd = fwd_in.astype(jnp.float32)
    nhat_fwd, _ = norm_rows(x_fwd)
    normed_fwd = (nhat_fwd * gain_row).astype(jnp.bfloat16)
    nhat_bwd, rstd_bwd = norm_rows(stash[0, 0].astype(jnp.float32))
    normed_bwd = (nhat_bwd * gain_row).astype(jnp.bfloat16)
    whole_fwd, whole_bwd, whole_cotan = (
        lax.all_gather(normed_fwd, "dp", axis=0, tiled=True),
        lax.all_gather(normed_bwd, "dp", axis=0, tiled=True),
        lax.all_gather(bwd_in, "dp", axis=0, tiled=True),
    )
    hidden_fwd = jnp.dot(whole_fwd, w_first, preferred_element_type=jnp.float32)
    acted_fwd = gelu_pair(hidden_fwd)[0].astype(jnp.bfloat16)
    hidden_bwd = jnp.dot(whole_bwd, w_first, preferred_element_type=jnp.float32)
    value_bwd, slope_bwd = gelu_pair(hidden_bwd)
    acted_bwd = value_bwd.astype(jnp.bfloat16)
    d_acted = jnp.dot(whole_cotan, w_second.T, preferred_element_type=jnp.float32)
    d_hidden = (d_acted * slope_bwd).astype(jnp.bfloat16)
    piece = acted_fwd
    branch_sum = lax.psum_scatter(
        jnp.dot(piece, w_second, preferred_element_type=jnp.float32),
        "dp",
        scatter_dimension=0,
        tiled=True,
    )
    piece = d_hidden
    d_normed = lax.psum_scatter(
        jnp.dot(piece, w_first.T, preferred_element_type=jnp.float32),
        "dp",
        scatter_dimension=0,
        tiled=True,
    )
    fwd_result = (x_fwd + branch_sum).astype(jnp.bfloat16)
    scaled = d_normed * gain_row
    d_input = rstd_bwd * (
        scaled
        - jnp.mean(scaled, axis=-1, keepdims=True)
        - nhat_bwd * jnp.mean(scaled * nhat_bwd, axis=-1, keepdims=True)
    )
    bwd_result = (bwd_in.astype(jnp.float32) + d_input).astype(jnp.bfloat16)
    half_width = w_first.shape[0] // 2
    own_start = mirror_pos * half_width
    other_start = (1 - mirror_pos) * half_width
    grad_first = rounded(jnp.dot(whole_bwd.T, d_hidden, preferred_element_type=jnp.float32))
    summed_first = lax.psum_scatter(
        grad_first.astype(jnp.bfloat16), "mirror", scatter_dimension=0, tiled=True
    )
    outgoing = (acted_bwd, lax.dynamic_slice_in_dim(whole_cotan, other_start, half_width, 1))
    far_acted, far_cotan = swapped((outgoing[0], outgoing[1]), "mirror", 0)
    own_second = jnp.dot(
        acted_bwd.T,
        lax.dynamic_slice_in_dim(whole_cotan, own_start, half_width, 1),
        preferred_element_type=jnp.float32,
    )
    far_second = jnp.dot(far_acted.T, far_cotan, preferred_element_type=jnp.float32)
    summed_second = rounded(own_second) + rounded(far_second)
    return (
        fwd_result[None, None],
        bwd_result[None, None],
        summed_first[None],
        summed_second.astype(jnp.bfloat16)[None],
    )


def solution(mesh):
    in_specs = (
        P("section", "mirror", "dp", None),
        P("section", "mirror", "dp", None),
        P("section", "mirror", "dp", None),
        P("section", None),
        P("section", None, "dp"),
        P("section", "dp", None),
    )
    out_specs = (
        P("section", "mirror", "dp", None),
        P("section", "mirror", "dp", None),
        P("section", "mirror", "dp"),
        P("section", "dp", "mirror"),
    )
    return jax.shard_map(
        on_device, mesh=mesh, in_specs=in_specs, out_specs=out_specs, check_vma=False
    )
```

profile of v0, /device:TPU:0, one launch (start us, length us, event | category | flops | bytes accessed | tf_op | source)
XLA Modules:
  0.0 135.8 jit_solution(11940512752795791094)
XLA Ops:
  8.0 0.0 copy-start
  8.0 0.0 copy-start.1
  8.0 0.0 all-reduce.5.cloned.1.call-start
  8.1 0.9 fusion.21
  9.0 3.0 %collective-permute-start.1 = (bf16[1,1,4096]{2,1,0:T(2,128)(2,1)S(1)}, bf16[1,1,4096]{2,1,0:T(2,128)(2,1)S(1)}, u32[]{:S(2)}, u32[]{:S(2)}) collective-permute-start(bf16[1,1,4096]{2,1,0:T(2,128)(2,1)S(1)} %get-tuple-element.13), channel_id=1, source_target_pairs={{16,0},{0,16},{17,1},{1,17},{18,2},{2,18},{19,3},{3,19},{20,4},{4,... | collective-permute-start | bytes 24584 | tf_op jit(solution)/shard_map/ppermute | solution.py:16
  12.0 0.1 collective-permute-start
  12.1 1.4 convert_reduce_fusion
  14.1 1.4 %multiply_reduce_fusion = f32[]{:T(128)} fusion(bf16[1,1,1,4096]{3,2,1,0:T(2,128)(2,1)} %param.8, f32[]{:T(128)S(6)} %div.20), kind=kLoop, calls=%fused_computation.49 | loop fusion | flops 16383 | bytes 8200 | tf_op jit(solution)/shard_map/reduce_sum | solution.py:29
  16.1 1.3 dynamic-slice.2
  17.4 0.0 collective-permute-done.1
  17.4 0.0 collective-permute-done
  17.4 0.6 fusion.59
  18.7 0.6 multiply_reduce_fusion.1
  20.0 0.8 fusion.27
  20.8 14.7 %all-gather.1 = bf16[8,1,4096]{2,1,0:T(2,128)(2,1)S(1)} all-gather(bf16[1,1,4096]{2,1,0:T(2,128)(2,1)S(1)} %get-tuple-element.16), channel_id=1, replica_groups=mesh['section'=2,'mirror'=2,'dp'=8] {'dp'}, dimensions={0}, use_global_device_ids=true | all-gather | bytes 73728 | tf_op jit(solution)/shard_map/all_gather | solution.py:70
  35.6 14.0 %all-gather = bf16[8,1,4096]{2,1,0:T(2,128)(2,1)S(1)} all-gather(bf16[1,1,4096]{2,1,0:T(2,128)(2,1)S(1)} %broadcast_select_fusion.2), channel_id=2, replica_groups=mesh['section'=2,'mirror'=2,'dp'=8] {'dp'}, dimensions={0}, use_global_device_ids=true | all-gather | bytes 73728 | tf_op jit(solution)/shard_map/all_gather | solution.py:72
  49.5 14.0 %all-gather.2 = bf16[8,1,4096]{2,1,0:T(2,128)(2,1)S(1)} all-gather(bf16[1,1,4096]{2,1,0:T(2,128)(2,1)S(1)} %get-tuple-element.15), channel_id=1, replica_groups=mesh['section'=2,'mirror'=2,'dp'=8] {'dp'}, dimensions={0}, use_global_device_ids=true | all-gather | bytes 73728 | tf_op jit(solution)/shard_map/all_gather | solution.py:71
  63.5 0.0 copy-done
  63.5 0.3 multiply_convert_fusion
  63.8 0.0 copy-done.1
  63.8 1.2 fusion.2
  65.0 0.4 fusion
  65.4 1.0 fusion.4
  66.4 0.0 all-reduce.5.cloned.1.call-update
  66.5 0.0 reduce-scatter.2.cloned.1.call-start
  66.5 1.5 %convolution_convert_fusion = bf16[4096,128]{1,0:T(8,128)(2,1)} fusion(bf16[8,128]{1,0:T(8,128)(2,1)S(1)} %fusion, bf16[8,1,4096]{2,1,0:T(2,128)(2,1)S(1)} %all-gather.2), kind=kOutput, calls=%fused_computation | convolution fusion | flops 8912896 | bytes 1116160 | tf_op jit(solution)/shard_map/dot_general | solution.py:106
  68.0 1.5 %collective-permute-start.2 = (bf16[8,128]{1,0:T(8,128)(2,1)S(1)}, bf16[8,128]{1,0:T(8,128)(2,1)S(1)}, u32[]{:S(2)}, u32[]{:S(2)}) collective-permute-start(bf16[8,128]{1,0:T(8,128)(2,1)S(1)} %get-tuple-element.17), channel_id=1, source_target_pairs={{0,8},{8,0},{1,9},{9,1},{2,10},{10,2},{3,11},{11,3},{4,12},{12,4},... | collective-permute-start | bytes 6152 | tf_op jit(solution)/shard_map/ppermute | solution.py:24
  69.6 0.0 reduce-scatter.2.cloned.1.call-update
  69.6 0.1 constant_dynamic-slice_fusion.1
  69.8 0.6 collective-permute-start.3
  70.3 0.3 convolution_convert_fusion.2
  70.7 0.0 copy-start.2
  70.7 0.0 copy-start.3
  70.7 0.9 collective-permute-done.2
  71.6 2.1 %collective-permute-done.3 = bf16[8,2048]{1,0:T(8,128)(2,1)S(1)} collective-permute-done((bf16[8,2048]{1,0:T(8,128)(2,1)S(1)}, bf16[8,2048]{1,0:T(8,128)(2,1)S(1)}, u32[]{:S(2)}, u32[]{:S(2)}) %collective-permute-start.3) | collective-permute-done | bytes 32800 | tf_op jit(solution)/shard_map/ppermute | solution.py:24
  73.7 0.3 convolution_convert_fusion.1
  74.1 0.9 fusion.10
  75.0 47.7 %all-reduce.5.cloned.1.call-done = (f32[8,4096]{1,0:T(8,128)}, f32[8,4096]{1,0:T(8,128)}) async-done(((f32[8,4096]{1,0:T(8,128)}, f32[8,4096]{1,0:T(8,128)}), (f32[8,4096]{1,0:T(8,128)}, f32[8,4096]{1,0:T(8,128)})) %all-reduce.5.cloned.1.call-update) | async-done | bytes 262160
  122.7 0.0 copy-done.2
  122.7 0.0 copy-done.3
  122.7 2.2 %fusion.58 = (f32[]{:T(128)}, f32[]{:T(128)}, f32[1,4096]{1,0:T(1,128)S(1)}) fusion(f32[]{:T(128)S(6)} %rsqrt.9, f32[]{:T(128)S(6)} %div.20, bf16[1,1,1,4096]{3,2,1,0:T(2,128)(2,1)S(1)} %copy-done.2, f32[1,4096]{1,0:T(1,128)S(1)} %copy-done.3, f32[8,4096]{1,0:T(8,128)} %get-tuple-element.7, u32[]{:T(128)} %bitcast.15), kind=kLoop, calls=%fused_computation.79 | loop fusion | flops 28670 | bytes 57364 | tf_op jit(solution)/shard_map/reduce_sum | solution.py:99
  126.2 2.2 %fusion.23 = (bf16[1,1,1,4096]{3,2,1,0:T(2,128)(2,1)}, bf16[1,1,1,4096]{3,2,1,0:T(2,128)(2,1)}) fusion(bf16[1,1,4096]{2,1,0:T(2,128)(2,1)S(1)} %broadcast_select_fusion.2, f32[1,4096]{1,0:T(1,128)S(1)} %get-tuple-element.8, f32[]{:T(128)S(6)} %div.23, f32[]{:T(128)S(6)} %div.22, f32[]{:T(128)S(6)} %rsqrt.9, f32[]{:T(128)S(6)} %div.20, ...), kind=kLoop, calls=%fused_computation.35 | loop fusion | flops 49152 | bytes 84484 | tf_op jit(solution)/shard_map/broadcast_in_dim | solution.py:121
  128.3 0.0 reduce-scatter.2.cloned.1.call-done
  (2 shorter events, 0.1 us)
Async XLA Ops:
  8.0 55.5 %copy-start = (bf16[1,4096,128]{2,1,0:T(8,128)(2,1)S(1)}, bf16[1,4096,128]{2,1,0:T(8,128)(2,1)}, u32[]{:S(2)}) copy-start(bf16[1,4096,128]{2,1,0:T(8,128)(2,1)} %param.10) | copy-start | bytes 3145732
  8.0 55.8 %copy-start.1 = (bf16[1,128,4096]{2,1,0:T(8,128)(2,1)S(1)}, bf16[1,128,4096]{2,1,0:T(8,128)(2,1)}, u32[]{:S(2)}) copy-start(bf16[1,128,4096]{2,1,0:T(8,128)(2,1)} %param.11) | copy-start | bytes 3145732
  8.0 114.7 %all-reduce.5.cloned.1.call-start = ((), (), s32[]{:S(2)}) async-start(), calls=%async_computation.2 | async-start | bytes 524288
  9.0 8.4 %collective-permute-start.1 = (bf16[1,1,4096]{2,1,0:T(2,128)(2,1)S(1)}, bf16[1,1,4096]{2,1,0:T(2,128)(2,1)S(1)}, u32[]{:S(2)}, u32[]{:S(2)}) collective-permute-start(bf16[1,1,4096]{2,1,0:T(2,128)(2,1)S(1)} %get-tuple-element.13), channel_id=1, source_target_pairs={{16,0},{0,16},{17,1},{1,17},{18,2},{2,18},{19,3},{3,19},{20,4},{4,... | collective-permute-start | bytes 24584 | tf_op jit(solution)/shard_map/ppermute | solution.py:16
  12.0 5.4 %collective-permute-start = (bf16[1,1,4096]{2,1,0:T(2,128)(2,1)S(1)}, bf16[1,1,4096]{2,1,0:T(2,128)(2,1)S(1)}, u32[]{:S(2)}, u32[]{:S(2)}) collective-permute-start(bf16[1,1,4096]{2,1,0:T(2,128)(2,1)S(1)} %get-tuple-element.14), channel_id=1, source_target_pairs={{0,16},{16,0},{1,17},{17,1},{2,18},{18,2},{3,19},{19,3},{4,20},{20... | collective-permute-start | bytes 24584 | tf_op jit(solution)/shard_map/ppermute | solution.py:13
  66.5 61.9 %reduce-scatter.2.cloned.1.call-start = ((), (), s32[]{:S(2)}) async-start(), calls=%async_computation.1 | async-start | bytes 1572864 | tf_op jit(solution)/shard_map/reduce_scatter | solution.py:107
  68.0 3.6 %collective-permute-start.2 = (bf16[8,128]{1,0:T(8,128)(2,1)S(1)}, bf16[8,128]{1,0:T(8,128)(2,1)S(1)}, u32[]{:S(2)}, u32[]{:S(2)}) collective-permute-start(bf16[8,128]{1,0:T(8,128)(2,1)S(1)} %get-tuple-element.17), channel_id=1, source_target_pairs={{0,8},{8,0},{1,9},{9,1},{2,10},{10,2},{3,11},{11,3},{4,12},{12,4},... | collective-permute-start | bytes 6152 | tf_op jit(solution)/shard_map/ppermute | solution.py:24
  69.8 4.0 %collective-permute-start.3 = (bf16[8,2048]{1,0:T(8,128)(2,1)S(1)}, bf16[8,2048]{1,0:T(8,128)(2,1)S(1)}, u32[]{:S(2)}, u32[]{:S(2)}) collective-permute-start(bf16[8,2048]{1,0:T(8,128)(2,1)S(1)} %bitcast.88), channel_id=1, source_target_pairs={{0,8},{8,0},{1,9},{9,1},{2,10},{10,2},{3,11},{11,3},{4,12},{12,4},... | collective-permute-start | bytes 98312 | tf_op jit(solution)/shard_map/ppermute | solution.py:24
  70.7 52.0 %copy-start.2 = (bf16[1,1,1,4096]{3,2,1,0:T(2,128)(2,1)S(1)}, bf16[1,1,1,4096]{3,2,1,0:T(2,128)(2,1)}, u32[]{:S(2)}) copy-start(bf16[1,1,1,4096]{3,2,1,0:T(2,128)(2,1)} %param.8) | copy-start | bytes 24580
  70.7 52.0 %copy-start.3 = (f32[1,4096]{1,0:T(1,128)S(1)}, f32[1,4096]{1,0:T(1,128)}, u32[]{:S(2)}) copy-start(f32[1,4096]{1,0:T(1,128)} %param.9) | copy-start | bytes 49156
Sparse Core Ops, SparseCore 0:
  66.6 56.0 all-reduce.4
Sparse Core Ops, SparseCore 1:
  69.8 21.2 reduce-scatter.1
where the time goes:
time: 136 us
  waiting for transfers between devices  50.7 us (37%)
  blocking collectives  42.7 us (31%)
  between operations  19.6 us (14%)
  other arithmetic  11 us (8%)
  starting transfers between devices  5.25 us (4%)
  matrix products  5.1 us (4%)
  local copies, waits for them, and re-layouts  1.47 us (1%)
    unnamed x3, waiting for transfers between devices  47.7 us
    all_gather x1, blocking collectives, on_device(): lax.all_gather(normed_fwd, 'dp', axis=0, tiled=True)  14.7 us
    all_gather x1, blocking collectives, on_device(): lax.all_gather(bwd_in, 'dp', axis=0, tiled=True)  14 us
    all_gather x1, blocking collectives, on_device(): lax.all_gather(normed_bwd, 'dp', axis=0, tiled=True)  14 us
    ppermute x2, waiting for transfers between devices, swapped(): return lax.ppermute(value, axis, pairs)  3.04 us
    ppermute x1, starting transfers between devices, extended_2(): lax.ppermute(lax.slice_in_dim(block, 0, width, axis=dim), axis, backward)  3 us
  transfers between devices with their start and end apart: 6, of which 3 were waited for; matrix products, arithmetic and copies ran while one was open for 9% of the time, Pallas kernels for 0%

commit v1 on v0

--- a/solution.py
+++ b/solution.py
@@ -2,6 +2,18 @@
 import jax.numpy as jnp
 from jax import lax
 from jax.sharding import PartitionSpec as P
+
+
+def collect(array, axis, dim):
+    ways, here, hop = (lax.axis_size(axis), lax.axis_index(axis), array.shape[dim])
+    line, have = (array, 1)
+    while have < ways:
+        line = jnp.concatenate(
+            [line, lax.ppermute(line, axis, [(d, (d - have) % ways) for d in range(ways)])],
+            axis=dim,
+        )
+        have = 2 * have
+    return jnp.roll(line, here * hop, axis=dim)
 
 
 def extended_2(block, sides, width):
@@ -69,7 +81,7 @@
     whole_fwd, whole_bwd, whole_cotan = (
         lax.all_gather(normed_fwd, "dp", axis=0, tiled=True),
         lax.all_gather(normed_bwd, "dp", axis=0, tiled=True),
-        lax.all_gather(bwd_in, "dp", axis=0, tiled=True),
+        collect(bwd_in, "dp", 0),
     )
     hidden_fwd = jnp.dot(whole_fwd, w_first, preferred_element_type=jnp.float32)
     acted_fwd = gelu_pair(hidden_fwd)[0].astype(jnp.bfloat16)

time: 136 us -> 130 us (0.956)
  blocking collectives: 42.7 us -> 28.8 us
  starting transfers between devices: 5.25 us -> 9.33 us
  waiting for transfers between devices: 50.7 us -> 53.3 us
    all_gather x1 -> x0, blocking collectives: 14 us -> none  [on_device(): lax.all_gather(bwd_in, 'dp', axis=0, tiled=True)]
    ppermute x0 -> x3, waiting for transfers between devices: none -> 4.36 us  [collect(): lax.ppermute(line, axis, [(d, (d - have) % ways) for d in range(ways)])]
    ppermute x0 -> x3, starting transfers between devices: none -> 4.1 us  [collect(): lax.ppermute(line, axis, [(d, (d - have) % ways) for d in range(ways)])]
    ppermute x1, starting transfers between devices: 3 us -> 0.08 us  [extended_2(): lax.ppermute(lax.slice_in_dim(block, 0, width, axis=dim), axis, backward)]
    ppermute x1, starting transfers between devices: 0.08 us -> 3 us  [extended_2(): lax.ppermute(lax.slice_in_dim(block, block.shape[dim] - width, None, axis...]
    unnamed x3, waiting for transfers between devices: 47.7 us -> 45.9 us
  transfers between devices with their start and end apart: 6 -> 9, of which waited for: 3 -> 4; matrix products, arithmetic and copies ran while one was open for 9% -> 11% of each run, Pallas kernels for 0% -> 0%
where the time goes in v1:
time: 130 us; the launch traced here: 129 us
  waiting for transfers between devices  53.3 us (41%)
  blocking collectives  28.8 us (22%)
  between operations  19.6 us (15%)
  other arithmetic  11.1 us (9%)
  starting transfers between devices  9.33 us (7%)
  matrix products  6.33 us (5%)
    unnamed x3, waiting for transfers between devices  45.9 us
    all_gather x1, blocking collectives, on_device(): lax.all_gather(normed_fwd, 'dp', axis=0, tiled=True)  14.7 us
    all_gather x1, blocking collectives, on_device(): lax.all_gather(normed_bwd, 'dp', axis=0, tiled=True)  14.1 us
    ppermute x3, waiting for transfers between devices, collect(): lax.ppermute(line, axis, [(d, (d - have) % ways) for d in range(ways)])  4.36 us
    ppermute x3, starting transfers between devices, collect(): lax.ppermute(line, axis, [(d, (d - have) % ways) for d in range(ways)])  4.1 us
    ppermute x2, waiting for transfers between devices, swapped(): return lax.ppermute(value, axis, pairs)  3.02 us
    ppermute x1, starting transfers between devices, extended_2(): lax.ppermute(lax.slice_in_dim(block, block.shape[dim] - width, None, axis...  3 us
  transfers between devices with their start and end apart: 9, of which 4 were waited for; matrix products, arithmetic and copies ran while one was open for 11% of the time, Pallas kernels for 0%

profile of v1, /device:TPU:0, one launch (start us, length us, event | category | flops | bytes accessed | tf_op | source)
XLA Modules:
  0.0 129.4 jit_solution(7851458815520455005)
XLA Ops:
  8.0 0.0 copy-start
  8.0 0.0 all-reduce.5.cloned.1.call-start
  8.1 0.9 fusion.22
  8.9 3.0 %collective-permute-start = (bf16[1,1,4096]{2,1,0:T(2,128)(2,1)S(1)}, bf16[1,1,4096]{2,1,0:T(2,128)(2,1)S(1)}, u32[]{:S(2)}, u32[]{:S(2)}) collective-permute-start(bf16[1,1,4096]{2,1,0:T(2,128)(2,1)S(1)} %get-tuple-element.12), channel_id=1, source_target_pairs={{0,16},{16,0},{1,17},{17,1},{2,18},{18,2},{3,19},{19,3},{4,20},{20... | collective-permute-start | bytes 24584 | tf_op jit(solution)/shard_map/ppermute | solution.py:25
  11.9 0.1 collective-permute-start.1
  12.0 1.4 %convert_reduce_fusion = f32[]{:T(128)} fusion(bf16[1,1,1,4096]{3,2,1,0:T(2,128)(2,1)} %param.8), kind=kLoop, calls=%fused_computation.51 | loop fusion | flops 8191 | bytes 8196 | tf_op jit(solution)/shard_map/reduce_sum | solution.py:40
  14.0 1.4 %multiply_reduce_fusion = f32[]{:T(128)} fusion(bf16[1,1,1,4096]{3,2,1,0:T(2,128)(2,1)} %param.8, f32[]{:T(128)S(6)} %div.20), kind=kLoop, calls=%fused_computation.49 | loop fusion | flops 16383 | bytes 8200 | tf_op jit(solution)/shard_map/reduce_sum | solution.py:41
  16.1 0.0 collective-permute-done
  16.1 0.0 collective-permute-done.1
  16.1 0.6 fusion.60
  17.4 0.6 multiply_reduce_fusion.1
  18.7 0.8 fusion.26
  19.5 14.7 %all-gather = bf16[8,1,4096]{2,1,0:T(2,128)(2,1)S(1)} all-gather(bf16[1,1,4096]{2,1,0:T(2,128)(2,1)S(1)} %get-tuple-element.14), channel_id=1, replica_groups=mesh['section'=2,'mirror'=2,'dp'=8] {'dp'}, dimensions={0}, use_global_device_ids=true | all-gather | bytes 73728 | tf_op jit(solution)/shard_map/all_gather | solution.py:82
  34.2 3.3 %collective-permute-start.2 = (bf16[1,4096]{1,0:T(2,128)(2,1)S(1)}, bf16[1,4096]{1,0:T(2,128)(2,1)S(1)}, u32[]{:S(2)}, u32[]{:S(2)}) collective-permute-start(bf16[1,4096]{1,0:T(2,128)(2,1)S(1)} %fusion.20), channel_id=1, source_target_pairs={{0,7},{1,0},{2,1},{3,2},{4,3},{5,4},{6,5},{7,6},{8,15},{9,8},{10,9... | collective-permute-start | bytes 24584 | tf_op jit(solution)/shard_map/ppermute | solution.py:12
  37.6 0.0 copy-done
  37.6 2.4 %fusion.2 = f32[8,4096]{1,0:T(8,128)} fusion(bf16[1,128,4096]{2,1,0:T(8,128)(2,1)} %param.11, bf16[1,4096,128]{2,1,0:T(8,128)(2,1)S(1)} %copy-done, bf16[8,1,4096]{2,1,0:T(2,128)(2,1)S(1)} %all-gather), kind=kOutput, calls=%fused_computation.6 | convolution fusion | flops 16786432 | bytes 2293760 | tf_op jit(solution)/shard_map/dot_general | solution.py:95
  40.0 0.0 collective-permute-done.2
  40.0 0.1 collective-permute-start.3
  40.2 14.1 %all-gather.1 = bf16[8,1,4096]{2,1,0:T(2,128)(2,1)S(1)} all-gather(bf16[1,1,4096]{2,1,0:T(2,128)(2,1)S(1)} %get-tuple-element.13), channel_id=1, replica_groups=mesh['section'=2,'mirror'=2,'dp'=8] {'dp'}, dimensions={0}, use_global_device_ids=true | all-gather | bytes 73728 | tf_op jit(solution)/shard_map/all_gather | solution.py:83
  54.3 0.0 collective-permute-done.3
  54.3 0.1 pad_maximum_fusion
  54.3 0.6 collective-permute-start.4
  55.0 0.3 multiply_convert_fusion
  55.3 4.3 %collective-permute-done.4 = bf16[4,4096]{1,0:T(4,128)(2,1)S(1)} collective-permute-done((bf16[4,4096]{1,0:T(4,128)(2,1)S(1)}, bf16[4,4096]{1,0:T(4,128)(2,1)S(1)}, u32[]{:S(2)}, u32[]{:S(2)}) %collective-permute-start.4) | collective-permute-done | bytes 32800 | tf_op jit(solution)/shard_map/ppermute | solution.py:12
  59.6 0.2 concatenate.16
  59.8 0.0 copy-done.1
  59.8 0.4 fusion
  60.2 1.0 fusion.4
  61.2 0.0 all-reduce.5.cloned.1.call-update
  61.3 0.0 copy-start.4
  61.3 0.0 reduce-scatter.2.cloned.1.call-start
  61.3 1.5 %convolution_convert_fusion = bf16[4096,128]{1,0:T(8,128)(2,1)} fusion(bf16[8,128]{1,0:T(8,128)(2,1)S(1)} %fusion, bf16[8,1,4096]{2,1,0:T(2,128)(2,1)S(1)} %all-gather.1), kind=kOutput, calls=%fused_computation | convolution fusion | flops 8912896 | bytes 1116160 | tf_op jit(solution)/shard_map/dot_general | solution.py:118
  62.8 0.0 reduce-scatter.2.cloned.1.call-update
  62.9 0.0 copy-done.4
  62.9 0.6 dynamic-slice
  63.5 1.5 %collective-permute-start.5 = (bf16[8,128]{1,0:T(8,128)(2,1)S(1)}, bf16[8,128]{1,0:T(8,128)(2,1)S(1)}, u32[]{:S(2)}, u32[]{:S(2)}) collective-permute-start(bf16[8,128]{1,0:T(8,128)(2,1)S(1)} %get-tuple-element.15), channel_id=1, source_target_pairs={{0,8},{8,0},{1,9},{9,1},{2,10},{10,2},{3,11},{11,3},{4,12},{12,4},... | collective-permute-start | bytes 6152 | tf_op jit(solution)/shard_map/ppermute | solution.py:36
  65.1 0.1 dynamic_slice.12
  65.1 0.6 collective-permute-start.6
  65.7 0.4 convolution_convert_fusion.2
  66.1 0.0 copy-start.2
  66.1 0.0 copy-start.3
  66.1 1.0 collective-permute-done.5
  67.1 2.0 %collective-permute-done.6 = bf16[8,2048]{1,0:T(8,128)(2,1)S(1)} collective-permute-done((bf16[8,2048]{1,0:T(8,128)(2,1)S(1)}, bf16[8,2048]{1,0:T(8,128)(2,1)S(1)}, u32[]{:S(2)}, u32[]{:S(2)}) %collective-permute-start.6) | collective-permute-done | bytes 32800 | tf_op jit(solution)/shard_map/ppermute | solution.py:36
  69.1 0.3 convolution_convert_fusion.1
  69.5 0.9 fusion.10
  70.4 45.9 %all-reduce.5.cloned.1.call-done = (f32[8,4096]{1,0:T(8,128)}, f32[8,4096]{1,0:T(8,128)}) async-done(((f32[8,4096]{1,0:T(8,128)}, f32[8,4096]{1,0:T(8,128)}), (f32[8,4096]{1,0:T(8,128)}, f32[8,4096]{1,0:T(8,128)})) %all-reduce.5.cloned.1.call-update) | async-done | bytes 262160
  116.3 2.2 %fusion.59 = (f32[]{:T(128)}, f32[]{:T(128)}, f32[1,4096]{1,0:T(1,128)S(1)}) fusion(f32[]{:T(128)S(6)} %rsqrt.9, f32[]{:T(128)S(6)} %div.20, bf16[1,1,1,4096]{3,2,1,0:T(2,128)(2,1)S(1)} %copy-done.2, f32[1,4096]{1,0:T(1,128)S(1)} %copy-done.3, f32[8,4096]{1,0:T(8,128)} %get-tuple-element.7, u32[]{:T(128)} %bitcast.13), kind=kLoop, calls=%fused_computation.78 | loop fusion | flops 28670 | bytes 57364 | tf_op jit(solution)/shard_map/reduce_sum | solution.py:111
  119.8 2.2 %fusion.24 = (bf16[1,1,1,4096]{3,2,1,0:T(2,128)(2,1)}, bf16[1,1,1,4096]{3,2,1,0:T(2,128)(2,1)}) fusion(f32[8,4096]{1,0:T(8,128)} %get-tuple-element.6, u32[]{:T(128)} %bitcast.13, f32[1,1,4096]{2,1,0:T(1,128)S(1)} %get-tuple-element.10, f32[]{:T(128)S(6)} %div.23, f32[]{:T(128)S(6)} %rsqrt.9, f32[]{:T(128)S(6)} %div.20, ...), kind=kLoop, calls=%fused_computation.37 | loop fusion | flops 49152 | bytes 84484 | tf_op jit(solution)/shard_map/broadcast_in_dim | solution.py:132
  (6 shorter events, 0.1 us)
Async XLA Ops:
  8.0 29.6 %copy-start = (bf16[1,4096,128]{2,1,0:T(8,128)(2,1)S(1)}, bf16[1,4096,128]{2,1,0:T(8,128)(2,1)}, u32[]{:S(2)}) copy-start(bf16[1,4096,128]{2,1,0:T(8,128)(2,1)} %param.10) | copy-start | bytes 3145732
  8.0 108.2 %all-reduce.5.cloned.1.call-start = ((), (), s32[]{:S(2)}) async-start(), calls=%async_computation.2 | async-start | bytes 524288
  8.9 7.2 %collective-permute-start = (bf16[1,1,4096]{2,1,0:T(2,128)(2,1)S(1)}, bf16[1,1,4096]{2,1,0:T(2,128)(2,1)S(1)}, u32[]{:S(2)}, u32[]{:S(2)}) collective-permute-start(bf16[1,1,4096]{2,1,0:T(2,128)(2,1)S(1)} %get-tuple-element.12), channel_id=1, source_target_pairs={{0,16},{16,0},{1,17},{17,1},{2,18},{18,2},{3,19},{19,3},{4,20},{20... | collective-permute-start | bytes 24584 | tf_op jit(solution)/shard_map/ppermute | solution.py:25
  11.9 4.2 %collective-permute-start.1 = (bf16[1,1,4096]{2,1,0:T(2,128)(2,1)S(1)}, bf16[1,1,4096]{2,1,0:T(2,128)(2,1)S(1)}, u32[]{:S(2)}, u32[]{:S(2)}) collective-permute-start(bf16[1,1,4096]{2,1,0:T(2,128)(2,1)S(1)} %get-tuple-element.11), channel_id=1, source_target_pairs={{16,0},{0,16},{17,1},{1,17},{18,2},{2,18},{19,3},{3,19},{20,4},{4,... | collective-permute-start | bytes 24584 | tf_op jit(solution)/shard_map/ppermute | solution.py:28
  34.2 5.7 %collective-permute-start.2 = (bf16[1,4096]{1,0:T(2,128)(2,1)S(1)}, bf16[1,4096]{1,0:T(2,128)(2,1)S(1)}, u32[]{:S(2)}, u32[]{:S(2)}) collective-permute-start(bf16[1,4096]{1,0:T(2,128)(2,1)S(1)} %fusion.20), channel_id=1, source_target_pairs={{0,7},{1,0},{2,1},{3,2},{4,3},{5,4},{6,5},{7,6},{8,15},{9,8},{10,9... | collective-permute-start | bytes 24584 | tf_op jit(solution)/shard_map/ppermute | solution.py:12
  40.0 19.8 %copy-start.1 = (bf16[1,128,4096]{2,1,0:T(8,128)(2,1)S(1)}, bf16[1,128,4096]{2,1,0:T(8,128)(2,1)}, u32[]{:S(2)}) copy-start(bf16[1,128,4096]{2,1,0:T(8,128)(2,1)} %param.11) | copy-start | bytes 3145732
  40.0 14.2 %collective-permute-start.3 = (bf16[2,4096]{1,0:T(2,128)(2,1)S(1)}, bf16[2,4096]{1,0:T(2,128)(2,1)S(1)}, u32[]{:S(2)}, u32[]{:S(2)}) collective-permute-start(bf16[2,4096]{1,0:T(2,128)(2,1)S(1)} %pad_maximum_fusion.1), channel_id=1, source_target_pairs={{0,6},{1,7},{2,0},{3,1},{4,2},{5,3},{6,4},{7,5},{8,14},{9,15},{10,... | collective-permute-start | bytes 49160 | tf_op jit(solution)/shard_map/ppermute | solution.py:12
  54.3 5.3 %collective-permute-start.4 = (bf16[4,4096]{1,0:T(4,128)(2,1)S(1)}, bf16[4,4096]{1,0:T(4,128)(2,1)S(1)}, u32[]{:S(2)}, u32[]{:S(2)}) collective-permute-start(bf16[4,4096]{1,0:T(4,128)(2,1)S(1)} %pad_maximum_fusion), channel_id=1, source_target_pairs={{0,4},{1,5},{2,6},{3,7},{4,0},{5,1},{6,2},{7,3},{8,12},{9,13},{10,... | collective-permute-start | bytes 98312 | tf_op jit(solution)/shard_map/ppermute | solution.py:12
  61.3 1.6 %copy-start.4 = (u32[32]{0:T(128)S(1)}, u32[32]{0:T(128)}, u32[]{:S(2)}) copy-start(u32[32]{0:T(128)} %constant.96) | copy-start | bytes 388
  61.3 60.7 %reduce-scatter.2.cloned.1.call-start = ((), (), s32[]{:S(2)}) async-start(), calls=%async_computation.1 | async-start | bytes 1572864 | tf_op jit(solution)/shard_map/reduce_scatter | solution.py:119
  63.5 3.6 %collective-permute-start.5 = (bf16[8,128]{1,0:T(8,128)(2,1)S(1)}, bf16[8,128]{1,0:T(8,128)(2,1)S(1)}, u32[]{:S(2)}, u32[]{:S(2)}) collective-permute-start(bf16[8,128]{1,0:T(8,128)(2,1)S(1)} %get-tuple-element.15), channel_id=1, source_target_pairs={{0,8},{8,0},{1,9},{9,1},{2,10},{10,2},{3,11},{11,3},{4,12},{12,4},... | collective-permute-start | bytes 6152 | tf_op jit(solution)/shard_map/ppermute | solution.py:36
  65.1 4.0 %collective-permute-start.6 = (bf16[8,2048]{1,0:T(8,128)(2,1)S(1)}, bf16[8,2048]{1,0:T(8,128)(2,1)S(1)}, u32[]{:S(2)}, u32[]{:S(2)}) collective-permute-start(bf16[8,2048]{1,0:T(8,128)(2,1)S(1)} %dynamic_slice.12), channel_id=1, source_target_pairs={{0,8},{8,0},{1,9},{9,1},{2,10},{10,2},{3,11},{11,3},{4,12},{12,4},... | collective-permute-start | bytes 98312 | tf_op jit(solution)/shard_map/ppermute | solution.py:36
  66.1 50.2 %copy-start.2 = (bf16[1,1,1,4096]{3,2,1,0:T(2,128)(2,1)S(1)}, bf16[1,1,1,4096]{3,2,1,0:T(2,128)(2,1)}, u32[]{:S(2)}) copy-start(bf16[1,1,1,4096]{3,2,1,0:T(2,128)(2,1)} %param.8) | copy-start | bytes 24580
  66.1 50.2 %copy-start.3 = (f32[1,4096]{1,0:T(1,128)S(1)}, f32[1,4096]{1,0:T(1,128)}, u32[]{:S(2)}) copy-start(f32[1,4096]{1,0:T(1,128)} %param.9) | copy-start | bytes 49156
Sparse Core Ops, SparseCore 0:
  61.4 54.8 all-reduce.4
Sparse Core Ops, SparseCore 1:
  64.7 19.9 reduce-scatter.1
